TPU v7x, 512 devices: a whole 4x4x16 slice. The times are simulated.
512 devices in a mesh: row: 128 (over x, z_hi, y, core), col: 4 (over z_lo).
Axes of the slice: x: 4, y: 4, z: 16 (z_hi: 4, z_lo: 4; z = z_hi * 4 + z_lo), core: 2. Of those that a mesh axis runs over, the one named last changes fastest.
Arguments:
- diag_inverse: float32 [512, 512], replicated, may hold values from -1 to 2, as said below
- panel: float32 [12288, 512], P('row', 'col'), may hold values from -0.3 to 0.3
- trailing: float32 [12288, 12288], P('row', 'col'), may hold values from -6 to 6
- agg_vals: float32 [128, 4, 192, 1024], P('row', 'col'), may hold values from -6 to 6
- agg_dest: int32 [128, 4, 192, 1], P('row', 'col'), may hold values from 0 to 127; in each aligned block of 192 rows (0 to 191, 192 to 383, ..., all dimensions but the last counted through in order) at most 2 rows name the same one
- agg_tile: int32 [128, 4, 192], P('row', 'col'), may hold values from 0 to 287
Outputs:
- updated: float32 [12288, 12288], P('row', 'col')
- panel_factor: float32 [12288, 512], P('row', 'col')
Inputs may be any that keep to these rules, and one draw needn't show every extreme that they name: `diag_inverse`: lower triangular with diagonal entries between 0.5 and 2. `agg_dest`: among the aggregates of one device no row index is named more than 2 times, and in some device one is named exactly 2 times.
All inputs are finite; a program needn't handle non-finite values.
Results may differ from a plain program's by a relative error of at most 0.000071.
Values sent between devices are 32-bit elements; how exact they have to be, the bound alone decides.
A program may use at most 64 MiB of HBM per device.

v0:
```python
import jax
import jax.numpy as jnp
from jax import lax
from jax.sharding import PartitionSpec as P

TILE_ROWS = 8
TILE_COLS = 128
CAP = 2


def per_device(diag_inverse, panel, trailing, agg_vals, agg_dest, agg_tile):
    row_devices = lax.axis_size("row")
    col_devices = lax.axis_size("col")
    local_rows, local_cols = trailing.shape
    panel_width = diag_inverse.shape[0]
    part_width = panel_width // col_devices
    col_index = lax.axis_index("col")
    contract_last = (((1,), (1,)), ((), ()))
    panel_whole = lax.all_gather(panel, "col", axis=1, tiled=True)
    own_full = jnp.dot(
        panel_whole,
        diag_inverse.T,
        precision=lax.Precision.HIGHEST,
        preferred_element_type=jnp.float32,
    )
    own_block = lax.dynamic_slice_in_dim(own_full, col_index * part_width, part_width, 1)
    column_all = lax.all_gather(own_block, "row", axis=0, tiled=True)
    split_rows = column_all.reshape(col_devices, local_cols, part_width)
    swapped = lax.all_to_all(split_rows, "col", split_axis=0, concat_axis=2, tiled=True)
    partner = swapped.reshape(local_cols, panel_width)
    tile_rows = local_rows // TILE_ROWS
    tile_cols = local_cols // TILE_COLS
    tiles_dev = tile_rows * tile_cols
    tile_values = agg_vals.reshape(agg_vals.shape[2], agg_vals.shape[3])
    targets = agg_dest.reshape(-1)
    tile_ids = agg_tile.reshape(-1)
    matches = (targets[:, None] == jnp.arange(row_devices, dtype=jnp.int32)[None, :]).astype(
        jnp.int32
    )
    earlier = jnp.cumsum(matches, axis=0) - matches
    ranks = jnp.sum(earlier * matches, axis=1)
    position = targets * CAP + ranks
    send_values = (
        jnp.zeros((row_devices * CAP, tile_values.shape[1]), jnp.float32)
        .at[position]
        .set(tile_values)
    )
    send_ids = (
        jnp.full((row_devices * CAP,), float(tiles_dev), jnp.float32)
        .at[position]
        .set(tile_ids.astype(jnp.float32))
    )
    got_values, got_ids = (
        lax.all_to_all(send_values, "row", split_axis=0, concat_axis=0, tiled=True),
        lax.all_to_all(send_ids, "row", split_axis=0, concat_axis=0, tiled=True),
    )
    landing = got_ids.astype(jnp.int32)
    blocked = trailing.reshape(tile_rows, TILE_ROWS, tile_cols, TILE_COLS)
    blocked = blocked.at[landing // tile_cols, :, landing % tile_cols, :].add(
        got_values.reshape(-1, TILE_ROWS, TILE_COLS), mode="drop"
    )
    assembled = blocked.reshape(local_rows, local_cols)
    product = lax.dot_general(
        own_full,
        partner,
        contract_last,
        precision=lax.Precision.HIGHEST,
        preferred_element_type=jnp.float32,
    )
    updated = assembled - product
    return (updated, own_block)


def solution(mesh):
    in_specs = (
        P(),
        P("row", "col"),
        P("row", "col"),
        P("row", "col", None, None),
        P("row", "col", None, None),
        P("row", "col", None),
    )
    out_specs = (P("row", "col"), P("row", "col"))
    return jax.shard_map(
        per_device, mesh=mesh, in_specs=in_specs, out_specs=out_specs, check_vma=False
    )
```

profile of v0, /device:TPU:1, one launch (start us, length us, event | category | flops | bytes accessed | tf_op | source)
XLA Modules:
  0.0 355.4 jit_solution(15490305446457586598)
XLA Ops:
  7.2 0.8 copy-done.4
  8.1 13.3 %all_gather.6 = f32[96,512]{1,0:T(8,128)S(1)} all-gather(f32[96,128]{1,0:T(8,128)S(1)} %copy-done.4), channel_id=1, replica_groups=mesh['row'=128,'col'=4] {'col'}, dimensions={1}, use_global_device_ids=true | all-gather | bytes 245760 | tf_op jit(solution)/shard_map/all_gather | solution.py:19
  21.4 1.1 fusion.10
  22.5 0.6 constant_dynamic-slice_fusion
  23.5 0.2 fusion.6
  23.7 1.2 scatter_custom_fusion
  24.9 0.8 all_to_all.23
  25.7 23.4 %all-to-all-start = ((f32[128,2,1]{1,2,0:T(1,128)}), f32[128,2,1]{1,2,0:T(1,128)S(1)}, u32[]{:S(2)}, u32[]{:S(2)}) async-start(f32[128,2,1]{1,2,0:T(1,128)} %bitcast.10), calls=%async_computation | async-start | bytes 131072 | tf_op jit(solution)/shard_map/all_to_all | solution.py:55
  49.1 1.5 scatter_custom_fusion.1
  50.6 1.6 all_to_all.25
  52.2 13.9 %all-to-all-done = f32[128,2,1]{1,2,0:T(1,128)S(1)} async-done(((f32[128,2,1]{1,2,0:T(1,128)}), f32[128,2,1]{1,2,0:T(1,128)S(1)}, u32[]{:S(2)}, u32[]{:S(2)}) %all-to-all-start) | async-done | bytes 1056 | tf_op jit(solution)/shard_map/all_to_all | solution.py:55
  66.1 6.9 %all-to-all-start.1 = ((f32[128,2,1024]{2,1,0:T(2,128)}), f32[128,2,1024]{2,1,0:T(2,128)S(1)}, u32[]{:S(2)}, u32[]{:S(2)}) async-start(f32[128,2,1024]{2,1,0:T(2,128)} %all_to_all.25), calls=%async_computation.1 | async-start | bytes 2097152 | tf_op jit(solution)/shard_map/all_to_all | solution.py:54
  73.0 117.3 %all-gather.2.cloned.1.call-done = f32[12288,128]{1,0:T(8,128)} async-done(((f32[96,128]{1,0:T(8,128)}), f32[12288,128]{1,0:T(8,128)}) %all-gather.2.cloned.1.call-update) | async-done | bytes 6291472 | tf_op jit(solution)/shard_map/all_gather | solution.py:27
  190.3 6.5 %copy.14 = f32[4,3072,128]{1,2,0:T(8,128)} copy(f32[4,3072,128]{2,1,0:T(8,128)} %bitcast.37) | data formatting | bytes 12582912 | tf_op jit(solution)/shard_map/reshape | solution.py:28
  196.8 1.0 copy-done.2
  197.8 5.4 %all-to-all-start.2 = ((f32[4,3072,128]{1,2,0:T(8,128)}), f32[4,3072,128]{1,2,0:T(8,128)}, u32[]{:S(2)}, u32[]{:S(2)}) async-start(f32[4,3072,128]{1,2,0:T(8,128)} %copy.14), calls=%async_computation.2 | async-start | bytes 12582912 | tf_op jit(solution)/shard_map/all_to_all | solution.py:29
  203.2 0.5 divide_reduce_fusion
  203.9 0.1 div.17
  204.0 0.3 compare_reduce_fusion
  204.3 0.1 ne.52
  204.5 2.1 reshape.174
  206.6 11.5 %scatter_fusion = f32[12,8,24,128]{3,1,2,0:T(8,128)S(1)} fusion(f32[12,8,24,128]{3,1,2,0:T(8,128)S(1)} %bitcast.36, s32[256]{0:T(256)S(1)} %bitcast.35, f32[256,8,128]{2,1,0:T(8,128)S(1)} %reshape.174), kind=kCustom, calls=%fused_computation.2 | custom fusion | flops 262144 | bytes 3147776 | tf_op jit(solution)/shard_map/scatter-add | solution.py:59
  218.1 123.0 %all-to-all-done.2 = f32[4,3072,128]{1,2,0:T(8,128)} async-done(((f32[4,3072,128]{1,2,0:T(8,128)}), f32[4,3072,128]{1,2,0:T(8,128)}, u32[]{:S(2)}, u32[]{:S(2)}) %all-to-all-start.2) | async-done | bytes 6291488 | tf_op jit(solution)/shard_map/all_to_all | solution.py:29
  341.1 7.5 %convolution_subtract_fusion = f32[96,3072]{1,0:T(8,128)} fusion(f32[96,512]{1,0:T(8,128)S(1)} %fusion.10, f32[3072,512]{0,1:T(8,128)} %bitcast.17, f32[12,8,24,128]{3,1,2,0:T(8,128)S(1)} %scatter_fusion), kind=kOutput, calls=%fused_computation.3 | convolution fusion | flops 1812234240 | bytes 8847360 | tf_op jit(solution)/shard_map/dot_general | solution.py:63
  (28 shorter events, 0.6 us)
Async XLA Ops:
  7.2 14.2 %copy-start = (f32[512,512]{1,0:T(8,128)S(1)}, f32[512,512]{1,0:T(8,128)}, u32[]{:S(2)}) copy-start(f32[512,512]{1,0:T(8,128)} %param.6) | copy-start | bytes 3145732
  7.2 0.9 copy-start.4
  7.2 183.1 %all-gather.2.cloned.1.call-start = ((), (), s32[]{:S(2)}) async-start(), calls=%async_computation.3 | async-start | bytes 6340608 | tf_op jit(solution)/shard_map/all_gather | solution.py:27
  7.2 15.9 %copy-start.5 = (s32[1,1,192,1]{2,3,1,0:T(1,128)S(1)}, s32[1,1,192,1]{2,3,1,0:T(1,128)}, u32[]{:S(2)}) copy-start(s32[1,1,192,1]{2,3,1,0:T(1,128)} %param.10) | copy-start | bytes 2308
  21.4 2.2 copy-start.6
  21.4 27.7 %copy-start.3 = (f32[1,1,192,1024]{3,2,1,0:T(8,128)S(1)}, f32[1,1,192,1024]{3,2,1,0:T(8,128)}, u32[]{:S(2)}) copy-start(f32[1,1,192,1024]{3,2,1,0:T(8,128)} %param.9) | copy-start | bytes 2359300
  25.7 40.4 %all-to-all-start = ((f32[128,2,1]{1,2,0:T(1,128)}), f32[128,2,1]{1,2,0:T(1,128)S(1)}, u32[]{:S(2)}, u32[]{:S(2)}) async-start(f32[128,2,1]{1,2,0:T(1,128)} %bitcast.10), calls=%async_computation | async-start | bytes 131072 | tf_op jit(solution)/shard_map/all_to_all | solution.py:55
  66.1 130.7 %all-to-all-start.1 = ((f32[128,2,1024]{2,1,0:T(2,128)}), f32[128,2,1024]{2,1,0:T(2,128)S(1)}, u32[]{:S(2)}, u32[]{:S(2)}) async-start(f32[128,2,1024]{2,1,0:T(2,128)} %all_to_all.25), calls=%async_computation.1 | async-start | bytes 2097152 | tf_op jit(solution)/shard_map/all_to_all | solution.py:54
  196.8 1.0 copy-start.2
  197.8 143.3 %all-to-all-start.2 = ((f32[4,3072,128]{1,2,0:T(8,128)}), f32[4,3072,128]{1,2,0:T(8,128)}, u32[]{:S(2)}, u32[]{:S(2)}) async-start(f32[4,3072,128]{1,2,0:T(8,128)} %copy.14), calls=%async_computation.2 | async-start | bytes 12582912 | tf_op jit(solution)/shard_map/all_to_all | solution.py:29
  203.7 2.9 copy-start.1
Sparse Core Ops, SparseCore 0:
  23.3 166.9 all-gather.1
where the time goes:
time: 356 us; the launch traced here: 355 us
  waiting for transfers between devices  254 us (71%)
  starting transfers between devices  35.7 us (10%)
  local copies, waits for them, and re-layouts  16.6 us (5%)
  between operations  14.2 us (4%)
  blocking collectives  13.3 us (4%)
  other arithmetic  12.8 us (4%)
  matrix products  8.63 us (2%)
    all_to_all x1, waiting for transfers between devices, per_device(): lax.all_to_all(split_rows, 'col', split_axis=0, concat_axis=2, tiled=True)  123 us
    all_gather x1, waiting for transfers between devices, per_device(): column_all = lax.all_gather(own_block, 'row', axis=0, tiled=True)  117 us
    all_to_all x1, starting transfers between devices, per_device(): lax.all_to_all(send_ids, 'row', split_axis=0, concat_axis=0, tiled=True)  23.4 us
    all_to_all x1, waiting for transfers between devices, per_device(): lax.all_to_all(send_ids, 'row', split_axis=0, concat_axis=0, tiled=True)  13.9 us
    all_gather x1, blocking collectives, per_device(): panel_whole = lax.all_gather(panel, 'col', axis=1, tiled=True)  13.3 us
    scatter-add x1, other arithmetic, per_device(): blocked.at[landing // tile_cols, :, landing % tile_cols, :]  11.5 us
    dot_general x1, matrix products, per_device(): lax.dot_general(own_full, partner, contract_last, precision=lax.Precision...  7.5 us
  transfers between devices with their start and end apart: 4, of which 3 were waited for; matrix products, arithmetic and copies ran while one was open for 7% of the time, Pallas kernels for 0%

commit v1 on v0

--- a/solution.py
+++ b/solution.py
@@ -24,7 +24,9 @@
         preferred_element_type=jnp.float32,
     )
     own_block = lax.dynamic_slice_in_dim(own_full, col_index * part_width, part_width, 1)
-    column_all = lax.all_gather(own_block, "row", axis=0, tiled=True)
+    column_all = jnp.concatenate(
+        lax.all_to_all(jnp.stack([own_block] * lax.axis_size("row")), "row", 0, 0), axis=0
+    )
     split_rows = column_all.reshape(col_devices, local_cols, part_width)
     swapped = lax.all_to_all(split_rows, "col", split_axis=0, concat_axis=2, tiled=True)
     partner = swapped.reshape(local_cols, panel_width)

time: 356 us -> 561 us (1.58)
  blocking collectives: 13.3 us -> 351 us
  waiting for transfers between devices: 254 us -> 136 us
  between operations: 14.2 us -> 0.89 us
    all_to_all x0 -> x1, blocking collectives: none -> 296 us  [per_device(): lax.all_to_all(jnp.stack([own_block] * lax.axis_size('row')), 'row', 0, 0)]
    all_gather x1 -> x0, waiting for transfers between devices: 117 us -> none  [per_device(): column_all = lax.all_gather(own_block, 'row', axis=0, tiled=True)]
    all_gather x1, blocking collectives: 13.3 us -> 55.4 us  [per_device(): panel_whole = lax.all_gather(panel, 'col', axis=1, tiled=True)]
    all_to_all x0 -> x1, local copies, waits for them, and re-layouts: none -> 6.53 us  [per_device(): lax.all_to_all(split_rows, 'col', split_axis=0, concat_axis=2, tiled=True)]
    reshape x1 -> x0, local copies, waits for them, and re-layouts: 6.52 us -> none  [per_device(): split_rows = column_all.reshape(col_devices, local_cols, part_width)]
  transfers between devices with their start and end apart: 4 -> 3, of which waited for: 3 -> 2; matrix products, arithmetic and copies ran while one was open for 7% -> 3% of each run, Pallas kernels for 0% -> 0%
where the time goes in v1:
time: 561 us; the launch traced here: 560 us
  blocking collectives  351 us (63%)
  waiting for transfers between devices  136 us (24%)
  starting transfers between devices  35.1 us (6%)
  local copies, waits for them, and re-layouts  15.9 us (3%)
  other arithmetic  12.8 us (2%)
  matrix products  8.63 us (2%)
    all_to_all x1, blocking collectives, per_device(): lax.all_to_all(jnp.stack([own_block] * lax.axis_size('row')), 'row', 0, 0)  296 us
    all_to_all x1, waiting for transfers between devices, per_device(): lax.all_to_all(split_rows, 'col', split_axis=0, concat_axis=2, tiled=True)  122 us
    all_gather x1, blocking collectives, per_device(): panel_whole = lax.all_gather(panel, 'col', axis=1, tiled=True)  55.4 us
    all_to_all x1, starting transfers between devices, per_device(): lax.all_to_all(send_ids, 'row', split_axis=0, concat_axis=0, tiled=True)  23 us
    all_to_all x1, waiting for transfers between devices, per_device(): lax.all_to_all(send_ids, 'row', split_axis=0, concat_axis=0, tiled=True)  13.8 us
    scatter-add x1, other arithmetic, per_device(): blocked.at[landing // tile_cols, :, landing % tile_cols, :]  11.5 us
  transfers between devices with their start and end apart: 3, of which 2 were waited for; matrix products, arithmetic and copies ran while one was open for 3% of the time, Pallas kernels for 0%

profile of v1, /device:TPU:1, one launch (start us, length us, event | category | flops | bytes accessed | tf_op | source)
XLA Modules:
  0.0 560.3 jit_solution(2083762842664101898)
XLA Ops:
  0.7 0.7 copy-done.6
  1.8 0.2 fusion.6
  2.0 1.2 scatter_custom_fusion
  3.2 0.8 all_to_all.26
  3.9 23.0 %all-to-all-start = ((f32[128,2,1]{1,2,0:T(1,128)}), f32[128,2,1]{1,2,0:T(1,128)S(1)}, u32[]{:S(2)}, u32[]{:S(2)}) async-start(f32[128,2,1]{1,2,0:T(1,128)} %bitcast.10), calls=%async_computation | async-start | bytes 131072 | tf_op jit(solution)/shard_map/all_to_all | solution.py:57
  27.0 1.5 scatter_custom_fusion.1
  28.5 1.6 all_to_all.28
  30.1 13.8 %all-to-all-done = f32[128,2,1]{1,2,0:T(1,128)S(1)} async-done(((f32[128,2,1]{1,2,0:T(1,128)}), f32[128,2,1]{1,2,0:T(1,128)S(1)}, u32[]{:S(2)}, u32[]{:S(2)}) %all-to-all-start) | async-done | bytes 1056 | tf_op jit(solution)/shard_map/all_to_all | solution.py:57
  43.9 6.7 %all-to-all-start.1 = ((f32[128,2,1024]{2,1,0:T(2,128)}), f32[128,2,1024]{2,1,0:T(2,128)S(1)}, u32[]{:S(2)}, u32[]{:S(2)}) async-start(f32[128,2,1024]{2,1,0:T(2,128)} %all_to_all.28), calls=%async_computation.1 | async-start | bytes 2097152 | tf_op jit(solution)/shard_map/all_to_all | solution.py:56
  50.7 55.4 %all_gather.3 = f32[96,512]{1,0:T(8,128)S(1)} all-gather(f32[96,128]{1,0:T(8,128)S(1)} %copy-done.5), channel_id=1, replica_groups=mesh['row'=128,'col'=4] {'col'}, dimensions={1}, use_global_device_ids=true | all-gather | bytes 245760 | tf_op jit(solution)/shard_map/all_gather | solution.py:19
  106.0 1.1 fusion.10
  107.2 0.8 stack.2
  108.0 0.2 copy-done.2
  108.2 295.8 %all_to_all.38 = f32[128,96,128]{2,1,0:T(8,128)} all-to-all(f32[128,96,128]{2,1,0:T(8,128)S(1)} %stack.2), channel_id=1, replica_groups=mesh['row'=128,'col'=4] {'row'}, dimensions={0} | all-to-all | bytes 12582912 | tf_op jit(solution)/shard_map/all_to_all | solution.py:28
  404.0 5.4 all-to-all-start.3
  409.4 0.5 divide_reduce_fusion
  410.1 0.1 div.17
  410.3 0.3 compare_reduce_fusion
  410.6 0.1 ne.52
  410.7 2.1 reshape.172
  412.8 11.5 %scatter_fusion = f32[12,8,24,128]{3,1,2,0:T(8,128)S(1)} fusion(f32[12,8,24,128]{3,1,2,0:T(8,128)S(1)} %bitcast.37, s32[256]{0:T(256)S(1)} %bitcast.36, f32[256,8,128]{2,1,0:T(8,128)S(1)} %reshape.172), kind=kCustom, calls=%fused_computation.2 | custom fusion | flops 262144 | bytes 3147776 | tf_op jit(solution)/shard_map/scatter-add | solution.py:61
  424.3 122.0 %all-to-all-done.3 = f32[4,3072,128]{2,1,0:T(8,128)} async-done(((f32[4,3072,128]{2,1,0:T(8,128)}), f32[4,3072,128]{2,1,0:T(8,128)}, u32[]{:S(2)}, u32[]{:S(2)}) %all-to-all-start.3) | async-done | bytes 6291488 | tf_op jit(solution)/shard_map/all_to_all | solution.py:31
  546.3 6.5 %copy.16 = f32[1,3072,4,128]{1,3,2,0:T(8,128)} copy(f32[1,3072,4,128]{3,1,2,0:T(8,128)} %bitcast.16) | data formatting | bytes 12582912 | tf_op jit(solution)/shard_map/all_to_all | solution.py:31
  552.8 7.5 %convolution_subtract_fusion = f32[96,3072]{1,0:T(8,128)} fusion(f32[96,512]{1,0:T(8,128)S(1)} %fusion.10, f32[3072,512]{0,1:T(8,128)} %bitcast.35, f32[12,8,24,128]{3,1,2,0:T(8,128)S(1)} %scatter_fusion), kind=kOutput, calls=%fused_computation.3 | convolution fusion | flops 1812234240 | bytes 8847360 | tf_op jit(solution)/shard_map/dot_general | solution.py:65
  (29 shorter events, 0.5 us)
Async XLA Ops:
  0.6 105.4 %copy-start = (f32[512,512]{1,0:T(8,128)S(1)}, f32[512,512]{1,0:T(8,128)}, u32[]{:S(2)}) copy-start(f32[512,512]{1,0:T(8,128)} %param.6) | copy-start | bytes 3145732
  0.6 0.8 copy-start.6
  0.7 1.3 copy-start.7
  0.7 26.3 %copy-start.3 = (f32[1,1,192,1024]{3,2,1,0:T(8,128)S(1)}, f32[1,1,192,1024]{3,2,1,0:T(8,128)}, u32[]{:S(2)}) copy-start(f32[1,1,192,1024]{3,2,1,0:T(8,128)} %param.9) | copy-start | bytes 2359300
  3.9 40.0 %all-to-all-start = ((f32[128,2,1]{1,2,0:T(1,128)}), f32[128,2,1]{1,2,0:T(1,128)S(1)}, u32[]{:S(2)}, u32[]{:S(2)}) async-start(f32[128,2,1]{1,2,0:T(1,128)} %bitcast.10), calls=%async_computation | async-start | bytes 131072 | tf_op jit(solution)/shard_map/all_to_all | solution.py:57
  30.1 20.5 %copy-start.5 = (f32[96,128]{1,0:T(8,128)S(1)}, f32[96,128]{1,0:T(8,128)}, u32[]{:S(2)}) copy-start(f32[96,128]{1,0:T(8,128)} %param.7) | copy-start | bytes 147460
  43.9 63.3 %all-to-all-start.1 = ((f32[128,2,1024]{2,1,0:T(2,128)}), f32[128,2,1024]{2,1,0:T(2,128)S(1)}, u32[]{:S(2)}, u32[]{:S(2)}) async-start(f32[128,2,1024]{2,1,0:T(2,128)} %all_to_all.28), calls=%async_computation.1 | async-start | bytes 2097152 | tf_op jit(solution)/shard_map/all_to_all | solution.py:56
  107.2 0.8 copy-start.4
  107.2 1.0 copy-start.2
  404.0 142.3 %all-to-all-start.3 = ((f32[4,3072,128]{2,1,0:T(8,128)}), f32[4,3072,128]{2,1,0:T(8,128)}, u32[]{:S(2)}, u32[]{:S(2)}) async-start(f32[4,3072,128]{2,1,0:T(8,128)} %bitcast.34), calls=%async_computation.3 | async-start | bytes 12582912 | tf_op jit(solution)/shard_map/all_to_all | solution.py:31
  410.0 2.9 copy-start.1
